TPU v7x, 256 devices: a whole 4x4x8 slice. The times are simulated.
256 devices in a mesh: seq: 32 (over x, z), chan: 8 (over y, core).
Axes of the slice: x: 4, y: 4, z: 8, core: 2. Of those that a mesh axis runs over, the one named last changes fastest.
Arguments:
- query_rows: bfloat16 [8192, 2048], P('seq', 'chan'), may hold values from -6 to 6
- key_rows: bfloat16 [8192, 2048], P('seq', 'chan'), may hold values from -6 to 6
- value_rows: bfloat16 [8192, 2048], P('seq', 'chan'), may hold values from -6 to 6
- long_filter: float32 [8192, 2048], P('seq', 'chan'), may hold values from -2 to 2
- short_taps: float32 [3, 3, 2048], P(None, None, ('seq', 'chan')), may hold values from -3 to 3
- skip_gain: float32 [2048], P(('seq', 'chan')), may hold values from -3 to 3
- cotangent: bfloat16 [8192, 2048], P('seq', 'chan'), may hold values from -6 to 6
Outputs:
- gated_out: bfloat16 [8192, 2048], P('seq', 'chan')
- query_grad: bfloat16 [8192, 2048], P('seq', 'chan')
- key_grad: bfloat16 [8192, 2048], P('seq', 'chan')
- value_grad: bfloat16 [8192, 2048], P('seq', 'chan')
- filter_grad: float32 [8192, 2048], P('seq', 'chan')
- taps_grad: float32 [3, 3, 2048], P(None, None, 'chan')
- skip_grad: float32 [2048], P('chan')
All inputs are finite; a program needn't handle non-finite values.
Results may differ from a plain program's by a relative error of at most 0.00135.
Values may be sent and summed in bfloat16 or wider, within the bound.
A program may use at most 64 MiB of HBM per device.

v0:
```python
import math
import jax
import jax.numpy as jnp
from jax import lax
from jax.sharding import PartitionSpec as P

exact_dot = lax.Precision.HIGHEST


def from_behind(value, axis, by):
    length = lax.axis_size(axis)
    pairs = [(i, i + by) for i in range(length) if 0 <= i + by < length]
    return lax.ppermute(value, axis, pairs)


def angles(left_index, right_index, period):
    product = left_index[:, None] * right_index[None, :] % period
    return 2.0 * math.pi / period * product.astype(jnp.float32)


def source_transform(pieces, row_start, total):
    sources = pieces.shape[1]
    row_count = pieces.shape[2]
    source_index = jnp.arange(sources, dtype=jnp.int32)
    freq_index = jnp.arange(2 * sources, dtype=jnp.int32)
    theta = angles(source_index, freq_index, 2 * sources)
    real_part = jnp.einsum("fqrc,qk->fkrc", pieces, jnp.cos(theta), precision=exact_dot)
    imag_part = -jnp.einsum("fqrc,qk->fkrc", pieces, jnp.sin(theta), precision=exact_dot)
    row_index = row_start + jnp.arange(row_count, dtype=jnp.int32)
    twist = angles(freq_index, row_index, total)
    cosine = jnp.cos(twist)[None, :, :, None]
    sine = jnp.sin(twist)[None, :, :, None]
    return jnp.stack([real_part * cosine + imag_part * sine, imag_part * cosine - real_part * sine])


def row_transform(spectra, direction):
    length = spectra.shape[3]
    positions = jnp.arange(length, dtype=jnp.int32)
    theta = angles(positions, positions, length)
    cosine = jnp.cos(theta)
    sine = jnp.sin(theta)
    real_cos = jnp.einsum("femc,mk->fekc", spectra[0], cosine, precision=exact_dot)
    real_sin = jnp.einsum("femc,mk->fekc", spectra[0], sine, precision=exact_dot)
    imag_cos = jnp.einsum("femc,mk->fekc", spectra[1], cosine, precision=exact_dot)
    imag_sin = jnp.einsum("femc,mk->fekc", spectra[1], sine, precision=exact_dot)
    return jnp.stack([real_cos - direction * imag_sin, imag_cos + direction * real_sin])


def untwist(spectra, freq_start, total):
    freq_index = freq_start + jnp.arange(spectra.shape[2], dtype=jnp.int32)
    row_index = jnp.arange(spectra.shape[3], dtype=jnp.int32)
    twist = angles(freq_index, row_index, total)
    cosine = jnp.cos(twist)[None, :, :, None]
    sine = jnp.sin(twist)[None, :, :, None]
    return jnp.stack(
        [spectra[0] * cosine - spectra[1] * sine, spectra[1] * cosine + spectra[0] * sine]
    )


def source_sum(spectra, total):
    freqs = spectra.shape[2]
    theta = angles(
        jnp.arange(freqs // 2, dtype=jnp.int32), jnp.arange(freqs, dtype=jnp.int32), freqs
    )
    summed = jnp.einsum("fkrc,qk->fqrc", spectra[0], jnp.cos(theta), precision=exact_dot)
    summed = summed - jnp.einsum("fkrc,qk->fqrc", spectra[1], jnp.sin(theta), precision=exact_dot)
    return summed / total


def spectrum_split(fields):
    devices = lax.axis_size("seq")
    place = lax.axis_index("seq")
    nfields, row_count, channels = fields.shape
    share = row_count // devices
    total = 2 * devices * row_count
    mixed = source_transform(
        lax.all_to_all(
            fields.reshape(nfields, 1, row_count, channels),
            "seq",
            split_axis=2,
            concat_axis=1,
            tiled=True,
        ),
        place * share,
        total,
    )
    mixed = mixed.reshape(2, nfields, devices, 2, share, channels)
    return row_transform(
        lax.all_to_all(mixed, "seq", split_axis=2, concat_axis=4, tiled=True)[:, :, 0], -1.0
    )


def signal_split(spectra):
    devices = lax.axis_size("seq")
    place = lax.axis_index("seq")
    nfields = spectra.shape[1]
    row_count = spectra.shape[3]
    channels = spectra.shape[4]
    share = row_count // devices
    total = 2 * devices * row_count
    turned = untwist(row_transform(spectra, 1.0), 2 * place, total)
    turned = turned.reshape(2, nfields, 1, 2, devices, share, channels)
    pieces = lax.all_to_all(turned, "seq", split_axis=4, concat_axis=2, tiled=True)
    gathered = source_sum(pieces.reshape(2, nfields, 2 * devices, share, pieces.shape[6]), total)
    return lax.all_to_all(gathered, "seq", split_axis=1, concat_axis=2, tiled=True).reshape(
        nfields, row_count, channels
    )


def complex_product(left, right, conjugate):
    right_imag = -right[1] if conjugate else right[1]
    return jnp.stack(
        [left[0] * right[0] - left[1] * right_imag, left[0] * right_imag + left[1] * right[0]]
    )


def per_device(query_rows, key_rows, value_rows, long_filter, short_taps, skip_gain, cotangent):
    row_count, channels = query_rows.shape
    devices = lax.axis_size("seq")
    grad_scale = 1.0 / math.sqrt(row_count * devices)
    all_taps, all_gain = (
        lax.all_gather(short_taps, ("seq", "chan"), axis=2, tiled=True),
        lax.all_gather(skip_gain, ("seq", "chan"), axis=0, tiled=True),
    )
    start = lax.axis_index("chan") * channels
    tap_block = lax.dynamic_slice_in_dim(all_taps, start, channels, 2)
    skip_block = lax.dynamic_slice_in_dim(all_gain, start, channels, 0)
    streams = jnp.stack([query_rows, key_rows, value_rows])
    lower = from_behind(streams[:, row_count - 2 :, :], "seq", 1)
    extended = jnp.concatenate([lower, streams], axis=1).astype(jnp.float32)
    shorted = sum(
        (
            tap_block[:, offset, None, :] * extended[:, 2 - offset : 2 - offset + row_count]
            for offset in range(3)
        )
    )
    query_conv = shorted[0]
    key_conv = shorted[1]
    value_conv = shorted[2]
    product = key_conv * value_conv
    upstream = cotangent.astype(jnp.float32)
    gated_grad = upstream * query_conv
    spectra = spectrum_split(jnp.stack([product, long_filter]))
    prod_spec = spectra[:, 0]
    filt_spec = spectra[:, 1]
    conv_part = signal_split(complex_product(prod_spec, filt_spec, False)[:, None])[0]
    grad_spec = spectrum_split(gated_grad[None])[:, 0]
    back = signal_split(
        jnp.stack(
            [
                complex_product(grad_spec, filt_spec, True),
                complex_product(grad_spec, prod_spec, True),
            ],
            axis=1,
        )
    )
    corr_product = back[0]
    corr_filter = back[1]
    mixed_conv = conv_part + skip_block * product
    gated_out = (query_conv * mixed_conv).astype(jnp.bfloat16)
    query_conv_grad = upstream * mixed_conv
    product_grad = corr_product + skip_block * gated_grad
    filter_grad = grad_scale * corr_filter
    key_conv_grad = product_grad * value_conv
    value_conv_grad = product_grad * key_conv
    conv_grads = jnp.stack([query_conv_grad, key_conv_grad, value_conv_grad])
    upper = from_behind(conv_grads[:, :2, :], "seq", -1)
    ext_grads = jnp.concatenate([conv_grads, upper], axis=1)
    input_grads = sum(
        (
            tap_block[:, offset, None, :] * ext_grads[:, offset : offset + row_count]
            for offset in range(3)
        )
    ).astype(jnp.bfloat16)
    tap_terms = jnp.stack(
        [
            jnp.sum(conv_grads * extended[:, 2 - offset : 2 - offset + row_count], axis=1)
            for offset in range(3)
        ],
        axis=1,
    )
    skip_terms = jnp.sum(gated_grad * product, axis=0)
    tap_total, skip_total = lax.psum((tap_terms, skip_terms), "seq")
    return (
        gated_out,
        input_grads[0],
        input_grads[1],
        input_grads[2],
        filter_grad,
        grad_scale * tap_total,
        grad_scale * skip_total,
    )


def solution(mesh):
    in_specs = (
        P("seq", "chan"),
        P("seq", "chan"),
        P("seq", "chan"),
        P("seq", "chan"),
        P(None, None, ("seq", "chan")),
        P(("seq", "chan")),
        P("seq", "chan"),
    )
    out_specs = (
        P("seq", "chan"),
        P("seq", "chan"),
        P("seq", "chan"),
        P("seq", "chan"),
        P("seq", "chan"),
        P(None, None, "chan"),
        P("chan"),
    )
    return jax.shard_map(
        per_device, mesh=mesh, in_specs=in_specs, out_specs=out_specs, check_vma=False
    )
```

profile of v0, /device:TPU:8, one launch (start us, length us, event | category | flops | bytes accessed | tf_op | source)
XLA Modules:
  0.0 597.0 jit_solution(4957405621104877456)
XLA Ops:
  1.4 3.8 collective-permute-start
  5.2 0.8 copy.38
  6.0 83.8 %all_gather.6 = f32[3,3,2048]{1,0,2:T(4,128)} all-gather(f32[3,3,8]{1,0,2:T(4,128)S(1)} %copy.38), channel_id=1, replica_groups=mesh['seq'=32,'chan'=8] {'seq','chan'}, dimensions={2}, use_global_device_ids=true | all-gather | bytes 74016 | tf_op jit(solution)/shard_map/all_gather | solution.py:122
  89.7 2.1 constant_dynamic-slice_fusion.1
  93.4 1.0 copy.55
  94.4 7.2 %all-to-all-start.4 = ((f32[1,1,256,256]{3,1,0,2:T(1,128)}), f32[1,1,256,256]{3,1,0,2:T(1,128)S(1)}, u32[]{:S(2)}, u32[]{:S(2)}) async-start(f32[1,1,256,256]{3,1,0,2:T(1,128)} %copy.55), calls=%async_computation.4 | async-start | bytes 524288 | tf_op jit(solution)/shard_map/all_to_all | solution.py:77
  101.7 1.2 copy.42
  102.9 11.3 %all-to-all-done.4 = f32[1,1,256,256]{3,1,0,2:T(1,128)S(1)} async-done(((f32[1,1,256,256]{3,1,0,2:T(1,128)}), f32[1,1,256,256]{3,1,0,2:T(1,128)S(1)}, u32[]{:S(2)}, u32[]{:S(2)}) %all-to-all-start.4) | async-done | bytes 262176 | tf_op jit(solution)/shard_map/all_to_all | solution.py:77
  114.3 4.7 all-to-all-start
  119.9 0.8 multiply_add_fusion.1
  121.8 1.6 copy.78
  123.4 12.5 %all-to-all-done = f32[2,1,256,256]{3,0,1,2:T(2,128)S(1)} async-done(((f32[2,1,256,256]{3,0,1,2:T(2,128)}), f32[2,1,256,256]{3,0,1,2:T(2,128)S(1)}, u32[]{:S(2)}, u32[]{:S(2)}) %all-to-all-start) | async-done | bytes 524320 | tf_op jit(solution)/shard_map/all_to_all | solution.py:77
  135.9 5.8 all-to-all-start.5
  141.7 1.1 convolution_negate_fusion
  142.8 1.4 add_bitcast_fusion.1
  144.2 1.6 stack.117
  145.8 1.6 stack.118
  147.4 2.7 pad_maximum_fusion
  150.1 2.5 copy.74
  152.7 17.1 %all-to-all-done.5 = f32[2,1,32,2,8,256]{5,3,4,1,0,2:T(2,128)} async-done(((f32[2,1,32,2,8,256]{5,3,4,1,0,2:T(2,128)}), f32[2,1,32,2,8,256]{5,3,4,1,0,2:T(2,128)}, u32[]{:S(2)}, u32[]{:S(2)}) %all-to-all-start.5) | async-done | bytes 1048608 | tf_op jit(solution)/shard_map/all_to_all | solution.py:89
  169.8 4.9 all-to-all-start.1
  174.8 2.4 fusion.254
  177.2 47.1 %all-to-all-done.1 = f32[2,2,32,2,8,256]{5,3,4,1,0,2:T(2,128)S(1)} async-done(((f32[2,2,32,2,8,256]{5,3,4,1,0,2:T(2,128)}), f32[2,2,32,2,8,256]{5,3,4,1,0,2:T(2,128)S(1)}, u32[]{:S(2)}, u32[]{:S(2)}) %all-to-all-start.1) | async-done | bytes 2097184 | tf_op jit(solution)/shard_map/all_to_all | solution.py:89
  224.3 0.8 fusion.253
  225.2 2.0 fusion.23
  227.2 2.0 fusion.19
  229.2 2.1 fusion.5
  231.3 2.1 fusion.3
  233.6 1.6 fusion.45
  235.2 13.2 %fusion.49 = f32[256,2,256]{2,0,1:T(8,128)S(1)} fusion(f32[1,1,2,256,256]{4,3,2,1,0:T(8,128)S(1)} %get-tuple-element.40), kind=kOutput, calls=%fused_computation.91 | convolution fusion | flops 403570688 | bytes 1048576 | tf_op jit(solution)/shard_map/femc,mk->fekc/dot_general | solution.py:42
  248.4 1.6 fusion.12
  250.1 1.8 subtract_bitcast_fusion.2
  252.0 1.1 copy.75
  253.1 6.2 %all-to-all-start.2 = ((f32[2,1,1,2,32,8,256]{6,5,3,2,1,0,4:T(8,128)}), f32[2,1,1,2,32,8,256]{6,5,3,2,1,0,4:T(8,128)}, u32[]{:S(2)}, u32[]{:S(2)}) async-start(f32[2,1,1,2,32,8,256]{6,5,3,2,1,0,4:T(8,128)} %copy.75), calls=%async_computation.2 | async-start | bytes 2097152 | tf_op jit(solution)/shard_map/all_to_all | solution.py:103
  259.2 1.6 fusion.40
  260.9 2.7 fusion.11
  263.6 1.6 fusion.36
  265.2 2.0 fusion.32
  267.3 2.0 fusion.58
  269.4 2.0 fusion.79
  271.4 2.3 fusion
  273.7 2.3 subtract_bitcast_fusion
  276.2 1.6 copy.79
  277.8 9.7 %all-to-all-done.2 = f32[2,1,1,2,32,8,256]{6,5,3,2,1,0,4:T(8,128)} async-done(((f32[2,1,1,2,32,8,256]{6,5,3,2,1,0,4:T(8,128)}), f32[2,1,1,2,32,8,256]{6,5,3,2,1,0,4:T(8,128)}, u32[]{:S(2)}, u32[]{:S(2)}) %all-to-all-start.2) | async-done | bytes 1048608 | tf_op jit(solution)/shard_map/all_to_all | solution.py:103
  287.5 4.9 all-to-all-start.6
  292.4 1.3 fusion.255
  294.9 0.9 copy.54
  295.7 46.4 %all-to-all-done.6 = f32[2,2,1,2,32,8,256]{6,5,3,1,2,0,4:T(8,128)S(1)} async-done(((f32[2,2,1,2,32,8,256]{6,5,3,1,2,0,4:T(8,128)}), f32[2,2,1,2,32,8,256]{6,5,3,1,2,0,4:T(8,128)S(1)}, u32[]{:S(2)}, u32[]{:S(2)}) %all-to-all-start.6) | async-done | bytes 2097184 | tf_op jit(solution)/shard_map/all_to_all | solution.py:103
  342.1 6.0 %all-to-all-start.3 = ((f32[1,32,8,256]{3,2,0,1:T(8,128)}), f32[1,32,8,256]{3,2,0,1:T(8,128)S(1)}, u32[]{:S(2)}, u32[]{:S(2)}) async-start(f32[1,32,8,256]{3,2,0,1:T(8,128)} %copy.54), calls=%async_computation.3 | async-start | bytes 524288 | tf_op jit(solution)/shard_map/all_to_all | solution.py:105
  348.1 1.2 fusion.252
  349.3 1.5 copy.65
  350.8 1.9 squeeze.40
  352.7 2.7 copy.64
  355.4 2.9 squeeze.39
  358.4 1.9 fusion.118
  361.0 1.1 copy.66
  362.2 9.8 %all-to-all-start.7 = ((f32[2,32,8,256]{3,2,0,1:T(8,128)}), f32[2,32,8,256]{3,2,0,1:T(8,128)S(1)}, u32[]{:S(2)}, u32[]{:S(2)}) async-start(f32[2,32,8,256]{3,2,0,1:T(8,128)} %copy.66), calls=%async_computation.7 | async-start | bytes 1048576 | tf_op jit(solution)/shard_map/all_to_all | solution.py:105
  372.3 75.6 %all-reduce = f32[2048]{0:T(1024)S(1)} all-reduce(f32[2048]{0:T(1024)S(1)} %dynamic-update-slice), channel_id=1, replica_groups=mesh['seq'=32,'chan'=8] {'seq','chan'}, use_global_device_ids=true, to_apply=%add | all-reduce | flops 2048 | bytes 16384
  447.9 0.8 fusion.61
  448.8 1.3 collective-permute-start.1
  450.1 0.7 fusion.66
  450.8 3.5 collective-permute-done.1
  454.9 139.8 %all-reduce.1 = (f32[3,3,256]{2,0,1:T(4,128)S(1)}, f32[256]{0:T(256)S(1)}) all-reduce(f32[3,3,256]{2,0,1:T(4,128)S(1)} %pad_maximum_fusion.7, f32[256]{0:T(256)S(1)} %get-tuple-element.57), channel_id=1, replica_groups=mesh['seq'=32,'chan'=8] {'seq'}, use_global_device_ids=true, to_apply=%region_3.4 | all-reduce | flops 2560 | bytes 20480 | tf_op jit(solution)/shard_map/psum | solution.py:183
  595.9 0.7 slice_bitcast_fusion.3
  (62 shorter events, 9.0 us)
Async XLA Ops:
  1.4 91.1 %collective-permute-start = (bf16[3,2,256]{2,1,0:T(2,128)(2,1)S(1)}, bf16[3,2,256]{2,1,0:T(2,128)(2,1)S(1)}, u32[]{:S(2)}, u32[]{:S(2)}) collective-permute-start(bf16[3,2,256]{2,1,0:T(2,128)(2,1)S(1)} %pad_maximum_fusion.8), channel_id=1, source_target_pairs={{0,8},{8,16},{16,24},{24,32},{32,40},{40,48},{48,56},{56,64},{64,7... | collective-permute-start | bytes 9224 | tf_op jit(solution)/shard_map/ppermute | solution.py:13
  89.7 2.7 copy-start.4
  89.7 2.7 copy-start.5
  89.7 2.8 copy-start.6
  92.5 0.9 copy-start.7
  92.6 9.1 %copy-start.9 = (f32[256,256]{1,0:T(8,128)S(1)}, f32[256,256]{1,0:T(8,128)}, u32[]{:S(2)}) copy-start(f32[256,256]{1,0:T(8,128)} %param.10) | copy-start | bytes 786436
  93.4 9.5 %copy-start = (f32[3,256,256]{2,1,0:T(8,128)}, f32[3,256,256]{2,1,0:T(8,128)S(1)}, u32[]{:S(2)}) copy-start(f32[3,256,256]{2,1,0:T(8,128)S(1)} %multiply_add_fusion) | copy-start | bytes 2359300
  94.4 19.9 %all-to-all-start.4 = ((f32[1,1,256,256]{3,1,0,2:T(1,128)}), f32[1,1,256,256]{3,1,0,2:T(1,128)S(1)}, u32[]{:S(2)}, u32[]{:S(2)}) async-start(f32[1,1,256,256]{3,1,0,2:T(1,128)} %copy.55), calls=%async_computation.4 | async-start | bytes 524288 | tf_op jit(solution)/shard_map/all_to_all | solution.py:77
  114.3 21.6 %all-to-all-start = ((f32[2,1,256,256]{3,0,1,2:T(2,128)}), f32[2,1,256,256]{3,0,1,2:T(2,128)S(1)}, u32[]{:S(2)}, u32[]{:S(2)}) async-start(f32[2,1,256,256]{3,0,1,2:T(2,128)} %copy.42), calls=%async_computation | async-start | bytes 1048576 | tf_op jit(solution)/shard_map/all_to_all | solution.py:77
  135.9 33.9 %all-to-all-start.5 = ((f32[2,1,32,2,8,256]{5,3,4,1,0,2:T(2,128)}), f32[2,1,32,2,8,256]{5,3,4,1,0,2:T(2,128)}, u32[]{:S(2)}, u32[]{:S(2)}) async-start(f32[2,1,32,2,8,256]{5,3,4,1,0,2:T(2,128)} %copy.78), calls=%async_computation.5 | async-start | bytes 2097152 | tf_op jit(solution)/shard_map/all_to_all | solution.py:89
  145.8 1.6 copy-start.2
  169.8 54.5 %all-to-all-start.1 = ((f32[2,2,32,2,8,256]{5,3,4,1,0,2:T(2,128)}), f32[2,2,32,2,8,256]{5,3,4,1,0,2:T(2,128)S(1)}, u32[]{:S(2)}, u32[]{:S(2)}) async-start(f32[2,2,32,2,8,256]{5,3,4,1,0,2:T(2,128)} %copy.74), calls=%async_computation.1 | async-start | bytes 4194304 | tf_op jit(solution)/shard_map/all_to_all | solution.py:89
  253.1 34.5 %all-to-all-start.2 = ((f32[2,1,1,2,32,8,256]{6,5,3,2,1,0,4:T(8,128)}), f32[2,1,1,2,32,8,256]{6,5,3,2,1,0,4:T(8,128)}, u32[]{:S(2)}, u32[]{:S(2)}) async-start(f32[2,1,1,2,32,8,256]{6,5,3,2,1,0,4:T(8,128)} %copy.75), calls=%async_computation.2 | async-start | bytes 2097152 | tf_op jit(solution)/shard_map/all_to_all | solution.py:103
  259.2 4.3 copy-start.3
  287.5 54.6 %all-to-all-start.6 = ((f32[2,2,1,2,32,8,256]{6,5,3,1,2,0,4:T(8,128)}), f32[2,2,1,2,32,8,256]{6,5,3,1,2,0,4:T(8,128)S(1)}, u32[]{:S(2)}, u32[]{:S(2)}) async-start(f32[2,2,1,2,32,8,256]{6,5,3,1,2,0,4:T(8,128)} %copy.79), calls=%async_computation.6 | async-start | bytes 4194304 | tf_op jit(solution)/shard_map/all_to_all | solution.py:103
  342.1 20.1 %all-to-all-start.3 = ((f32[1,32,8,256]{3,2,0,1:T(8,128)}), f32[1,32,8,256]{3,2,0,1:T(8,128)S(1)}, u32[]{:S(2)}, u32[]{:S(2)}) async-start(f32[1,32,8,256]{3,2,0,1:T(8,128)} %copy.54), calls=%async_computation.3 | async-start | bytes 524288 | tf_op jit(solution)/shard_map/all_to_all | solution.py:105
  360.3 11.7 %copy-start.10 = (f32[8]{0:T(128)S(1)}, f32[8]{0:T(128)}, u32[]{:S(2)}) copy-start(f32[8]{0:T(128)} %param.12) | copy-start | bytes 100
  360.3 87.6 %copy-start.1 = (f32[3,256,256]{2,1,0:T(8,128)S(1)}, f32[3,256,256]{2,1,0:T(8,128)}, u32[]{:S(2)}) copy-start(f32[3,256,256]{2,1,0:T(8,128)} %copy-done) | copy-start | bytes 2359300
  360.3 87.6 %copy-start.8 = (bf16[256,256]{1,0:T(8,128)(2,1)S(1)}, bf16[256,256]{1,0:T(8,128)(2,1)}, u32[]{:S(2)}) copy-start(bf16[256,256]{1,0:T(8,128)(2,1)} %param.13) | copy-start | bytes 393220
  362.2 85.8 %all-to-all-start.7 = ((f32[2,32,8,256]{3,2,0,1:T(8,128)}), f32[2,32,8,256]{3,2,0,1:T(8,128)S(1)}, u32[]{:S(2)}, u32[]{:S(2)}) async-start(f32[2,32,8,256]{3,2,0,1:T(8,128)} %copy.66), calls=%async_computation.7 | async-start | bytes 1048576 | tf_op jit(solution)/shard_map/all_to_all | solution.py:105
  448.8 5.5 collective-permute-start.1
where the time goes:
time: 606 us; the launch traced here: 597 us
  blocking collectives  299 us (49%)
  waiting for transfers between devices  148 us (24%)
  starting transfers between devices  54.5 us (9%)
  matrix products  50.8 us (8%)
  local copies, waits for them, and re-layouts  35.4 us (6%)
  other arithmetic  7.9 us (1%)
    psum x1, blocking collectives, per_device(): tap_total, skip_total = lax.psum((tap_terms, skip_terms), 'seq')  140 us
    all_gather x1, blocking collectives, per_device(): lax.all_gather(short_taps, ('seq', 'chan'), axis=2, tiled=True)  83.8 us
    unnamed x1, blocking collectives  75.6 us
    all_to_all x2, waiting for transfers between devices, spectrum_split(): lax.all_to_all(mixed, 'seq', split_axis=2, concat_axis=4, tiled=True)  64.2 us
    all_to_all x2, waiting for transfers between devices, signal_split(): lax.all_to_all(turned, 'seq', split_axis=4, concat_axis=2, tiled=True)  56.1 us
    all_to_all x2, waiting for transfers between devices, spectrum_split(): lax.all_to_all(fields.reshape(nfields, 1, row_count, channels), 'seq', sp...  23.8 us
    dot_general x4, matrix products, row_transform(): jnp.einsum('femc,mk->fekc', spectra[0], cosine, precision=exact_dot)  18.9 us
    all_to_all x2, starting transfers between devices, signal_split(): lax.all_to_all(gathered, 'seq', split_axis=1, concat_axis=2, tiled=True)  15.8 us
  transfers between devices with their start and end apart: 10, of which 7 were waited for; matrix products, arithmetic and copies ran while one was open for 10% of the time, Pallas kernels for 0%

commit v1 on v0

--- a/solution.py
+++ b/solution.py
@@ -5,6 +5,12 @@
 from jax.sharding import PartitionSpec as P
 
 exact_dot = lax.Precision.HIGHEST
+
+
+def exchange_blocks(x, name, split, join):
+    pieces = jnp.split(x, lax.axis_size(name), axis=split)
+    received = lax.all_to_all(jnp.stack(pieces), name, 0, 0)
+    return jnp.concatenate(received, axis=join)
 
 
 def from_behind(value, axis, by):
@@ -100,7 +106,7 @@
     total = 2 * devices * row_count
     turned = untwist(row_transform(spectra, 1.0), 2 * place, total)
     turned = turned.reshape(2, nfields, 1, 2, devices, share, channels)
-    pieces = lax.all_to_all(turned, "seq", split_axis=4, concat_axis=2, tiled=True)
+    pieces = exchange_blocks(turned, "seq", 4, 2)
     gathered = source_sum(pieces.reshape(2, nfields, 2 * devices, share, pieces.shape[6]), total)
     return lax.all_to_all(gathered, "seq", split_axis=1, concat_axis=2, tiled=True).reshape(
         nfields, row_count, channels

time: 606 us -> 631 us (1.041)
  other arithmetic: 7.9 us -> 27.2 us
    unnamed x0 -> x62, other arithmetic: none -> 18.9 us
    all_to_all x2, waiting for transfers between devices: 56.1 us -> 67.1 us  [exchange_blocks(): received = lax.all_to_all(jnp.stack(pieces), name, 0, 0)]
    dot_general x4, matrix products: 18.9 us -> 8.29 us  [row_transform(): jnp.einsum('femc,mk->fekc', spectra[0], cosine, precision=exact_dot)]
    dot_general x4, matrix products: 8.88 us -> 16.6 us  [row_transform(): jnp.einsum('femc,mk->fekc', spectra[1], sine, precision=exact_dot)]
  transfers between devices with their start and end apart: 10 -> 10, of which waited for: 7 -> 7; matrix products, arithmetic and copies ran while one was open for 10% -> 8% of each run, Pallas kernels for 0% -> 0%
where the time goes in v1:
time: 631 us; the launch traced here: 622 us
  blocking collectives  299 us (47%)
  waiting for transfers between devices  154 us (24%)
  starting transfers between devices  54.5 us (9%)
  matrix products  51 us (8%)
  local copies, waits for them, and re-layouts  34.3 us (5%)
  other arithmetic  27.2 us (4%)
    psum x1, blocking collectives, per_device(): tap_total, skip_total = lax.psum((tap_terms, skip_terms), 'seq')  140 us
    all_gather x1, blocking collectives, per_device(): lax.all_gather(short_taps, ('seq', 'chan'), axis=2, tiled=True)  83.8 us
    unnamed x1, blocking collectives  75.6 us
    all_to_all x2, waiting for transfers between devices, exchange_blocks(): received = lax.all_to_all(jnp.stack(pieces), name, 0, 0)  67.1 us
    all_to_all x2, waiting for transfers between devices, spectrum_split(): lax.all_to_all(mixed, 'seq', split_axis=2, concat_axis=4, tiled=True)  59.5 us
    all_to_all x2, waiting for transfers between devices, spectrum_split(): lax.all_to_all(fields.reshape(nfields, 1, row_count, channels), 'seq', sp...  24 us
    unnamed x62, other arithmetic  18.9 us
    dot_general x4, matrix products, row_transform(): jnp.einsum('femc,mk->fekc', spectra[1], sine, precision=exact_dot)  16.6 us
  transfers between devices with their start and end apart: 10, of which 7 were waited for; matrix products, arithmetic and copies ran while one was open for 8% of the time, Pallas kernels for 0%

profile of v1, /device:TPU:8, one launch (start us, length us, event | category | flops | bytes accessed | tf_op | source)
XLA Modules:
  0.0 622.1 jit_solution(16646387764482466665)
XLA Ops:
  1.4 3.8 collective-permute-start
  5.2 0.8 copy.162
  6.0 83.8 %all_gather.6 = f32[3,3,2048]{1,0,2:T(4,128)} all-gather(f32[3,3,8]{1,0,2:T(4,128)S(1)} %copy.162), channel_id=1, replica_groups=mesh['seq'=32,'chan'=8] {'seq','chan'}, dimensions={2}, use_global_device_ids=true | all-gather | bytes 74016 | tf_op jit(solution)/shard_map/all_gather | solution.py:128
  89.8 2.2 constant_dynamic-slice_fusion.1
  93.6 1.0 copy.208
  94.5 7.1 %all-to-all-start.4 = ((f32[1,1,256,256]{3,1,0,2:T(1,128)}), f32[1,1,256,256]{3,1,0,2:T(1,128)S(1)}, u32[]{:S(2)}, u32[]{:S(2)}) async-start(f32[1,1,256,256]{3,1,0,2:T(1,128)} %copy.208), calls=%async_computation.4 | async-start | bytes 524288 | tf_op jit(solution)/shard_map/all_to_all | solution.py:83
  101.8 1.2 copy.166
  103.0 11.5 %all-to-all-done.4 = f32[1,1,256,256]{3,1,0,2:T(1,128)S(1)} async-done(((f32[1,1,256,256]{3,1,0,2:T(1,128)}), f32[1,1,256,256]{3,1,0,2:T(1,128)S(1)}, u32[]{:S(2)}, u32[]{:S(2)}) %all-to-all-start.4) | async-done | bytes 262176 | tf_op jit(solution)/shard_map/all_to_all | solution.py:83
  114.4 4.5 all-to-all-start
  119.8 0.8 multiply_add_fusion.1
  121.8 1.6 copy.259
  123.4 12.5 %all-to-all-done = f32[2,1,256,256]{3,0,1,2:T(2,128)S(1)} async-done(((f32[2,1,256,256]{3,0,1,2:T(2,128)}), f32[2,1,256,256]{3,0,1,2:T(2,128)S(1)}, u32[]{:S(2)}, u32[]{:S(2)}) %all-to-all-start) | async-done | bytes 524320 | tf_op jit(solution)/shard_map/all_to_all | solution.py:83
  135.9 5.7 all-to-all-start.5
  141.6 1.1 convolution_negate_fusion
  142.7 1.4 add_bitcast_fusion.1
  144.1 1.6 stack.315
  145.7 1.6 stack.316
  147.3 2.7 pad_maximum_fusion
  150.1 2.6 copy.256
  152.6 17.3 %all-to-all-done.5 = f32[2,1,32,2,8,256]{5,3,4,1,0,2:T(2,128)} async-done(((f32[2,1,32,2,8,256]{5,3,4,1,0,2:T(2,128)}), f32[2,1,32,2,8,256]{5,3,4,1,0,2:T(2,128)}, u32[]{:S(2)}, u32[]{:S(2)}) %all-to-all-start.5) | async-done | bytes 1048608 | tf_op jit(solution)/shard_map/all_to_all | solution.py:95
  169.9 4.9 all-to-all-start.1
  174.9 1.6 fusion.318
  176.5 1.6 fusion.40
  178.2 1.6 fusion.11
  179.8 2.4 fusion.36
  182.3 42.2 %all-to-all-done.1 = f32[2,2,32,2,8,256]{5,3,4,1,0,2:T(2,128)S(1)} async-done(((f32[2,2,32,2,8,256]{5,3,4,1,0,2:T(2,128)}), f32[2,2,32,2,8,256]{5,3,4,1,0,2:T(2,128)S(1)}, u32[]{:S(2)}, u32[]{:S(2)}) %all-to-all-start.1) | async-done | bytes 2097184 | tf_op jit(solution)/shard_map/all_to_all | solution.py:95
  224.5 0.8 fusion.317
  225.3 2.0 fusion.23
  227.3 2.0 fusion.19
  229.4 10.8 %fusion.5 = f32[1,2,2,256,256]{4,3,2,1,0:T(8,128)S(1)} fusion(f32[256,2,2,256]{3,0,2,1:T(8,128)S(1)} %fusion.23, f32[1,2,1,2,32,8,256]{6,3,5,1,0,4,2:T(2,128)S(1)} %get-tuple-element.42), kind=kOutput, calls=%fused_computation.137 | convolution fusion | flops 806748160 | bytes 3145728 | tf_op jit(solution)/shard_map/femc,mk->fekc/dot_general | solution.py:51
  240.2 2.1 fusion.3
  242.5 0.9 copy-done.6
  243.5 2.0 fusion.32
  245.6 3.0 fusion.58
  248.6 3.0 fusion.79
  251.6 1.6 fusion.45
  253.3 1.6 fusion.49
  254.9 1.8 fusion.12
  256.8 1.8 subtract_bitcast_fusion.2
  277.9 6.1 all-to-all-start.2
  284.1 3.4 fusion
  287.4 2.3 subtract_bitcast_fusion
  290.2 1.3 copy-done.4
  291.6 20.7 %all-to-all-done.2 = f32[32,2,1,1,2,1,8,256]{7,6,4,1,5,3,2,0:T(8,128)} async-done(((f32[32,2,1,1,2,1,8,256]{7,6,4,1,5,3,2,0:T(8,128)}), f32[32,2,1,1,2,1,8,256]{7,6,4,1,5,3,2,0:T(8,128)}, u32[]{:S(2)}, u32[]{:S(2)}) %all-to-all-start.2) | async-done | bytes 1048608 | tf_op jit(solution)/shard_map/all_to_all | solution.py:12
  312.3 4.9 all-to-all-start.6
  317.3 1.3 fusion.319
  319.7 0.9 copy.207
  320.5 46.4 %all-to-all-done.6 = f32[32,2,2,1,2,1,8,256]{7,6,4,2,1,5,3,0:T(8,128)S(1)} async-done(((f32[32,2,2,1,2,1,8,256]{7,6,4,2,1,5,3,0:T(8,128)}), f32[32,2,2,1,2,1,8,256]{7,6,4,2,1,5,3,0:T(8,128)S(1)}, u32[]{:S(2)}, u32[]{:S(2)}) %all-to-all-start.6) | async-done | bytes 2097184 | tf_op jit(solution)/shard_map/all_to_all | solution.py:12
  366.9 6.3 %all-to-all-start.3 = ((f32[1,32,8,256]{3,2,0,1:T(8,128)}), f32[1,32,8,256]{3,2,0,1:T(8,128)S(1)}, u32[]{:S(2)}, u32[]{:S(2)}) async-start(f32[1,32,8,256]{3,2,0,1:T(8,128)} %copy.207), calls=%async_computation.3 | async-start | bytes 524288 | tf_op jit(solution)/shard_map/all_to_all | solution.py:111
  373.2 1.2 fusion.316
  374.3 1.5 copy.247
  375.9 1.9 squeeze.40
  377.8 2.7 copy.246
  380.5 2.9 squeeze.39
  383.5 1.9 fusion.182
  386.1 1.1 copy.248
  387.2 9.9 %all-to-all-start.7 = ((f32[2,32,8,256]{3,2,0,1:T(8,128)}), f32[2,32,8,256]{3,2,0,1:T(8,128)S(1)}, u32[]{:S(2)}, u32[]{:S(2)}) async-start(f32[2,32,8,256]{3,2,0,1:T(8,128)} %copy.248), calls=%async_computation.7 | async-start | bytes 1048576 | tf_op jit(solution)/shard_map/all_to_all | solution.py:111
  397.4 75.6 %all-reduce = f32[2048]{0:T(1024)S(1)} all-reduce(f32[2048]{0:T(1024)S(1)} %dynamic-update-slice), channel_id=1, replica_groups=mesh['seq'=32,'chan'=8] {'seq','chan'}, use_global_device_ids=true, to_apply=%add | all-reduce | flops 2048 | bytes 16384
  473.1 0.8 fusion.61
  474.0 1.3 collective-permute-start.1
  475.3 0.7 fusion.66
  476.0 3.5 collective-permute-done.1
  480.1 139.6 %all-reduce.1 = (f32[3,3,256]{2,0,1:T(4,128)S(1)}, f32[256]{0:T(256)S(1)}) all-reduce(f32[3,3,256]{2,0,1:T(4,128)S(1)} %pad_maximum_fusion.7, f32[256]{0:T(256)S(1)} %get-tuple-element.57), channel_id=1, replica_groups=mesh['seq'=32,'chan'=8] {'seq'}, use_global_device_ids=true, to_apply=%region_3.4 | all-reduce | flops 2560 | bytes 20480 | tf_op jit(solution)/shard_map/psum | solution.py:189
  620.9 0.7 slice_bitcast_fusion.3
  (130 shorter events, 28.5 us)
Async XLA Ops:
  1.4 91.2 %collective-permute-start = (bf16[3,2,256]{2,1,0:T(2,128)(2,1)S(1)}, bf16[3,2,256]{2,1,0:T(2,128)(2,1)S(1)}, u32[]{:S(2)}, u32[]{:S(2)}) collective-permute-start(bf16[3,2,256]{2,1,0:T(2,128)(2,1)S(1)} %pad_maximum_fusion.8), channel_id=1, source_target_pairs={{0,8},{8,16},{16,24},{24,32},{32,40},{40,48},{48,56},{56,64},{64,7... | collective-permute-start | bytes 9224 | tf_op jit(solution)/shard_map/ppermute | solution.py:19
  89.8 2.8 copy-start.8
  89.8 2.8 copy-start.9
  89.8 2.8 copy-start.10
  92.6 0.9 copy-start.11
  92.7 9.0 %copy-start.13 = (f32[256,256]{1,0:T(8,128)S(1)}, f32[256,256]{1,0:T(8,128)}, u32[]{:S(2)}) copy-start(f32[256,256]{1,0:T(8,128)} %param.10) | copy-start | bytes 786436
  93.5 9.5 %copy-start = (f32[3,256,256]{2,1,0:T(8,128)}, f32[3,256,256]{2,1,0:T(8,128)S(1)}, u32[]{:S(2)}) copy-start(f32[3,256,256]{2,1,0:T(8,128)S(1)} %multiply_add_fusion) | copy-start | bytes 2359300
  94.5 19.9 %all-to-all-start.4 = ((f32[1,1,256,256]{3,1,0,2:T(1,128)}), f32[1,1,256,256]{3,1,0,2:T(1,128)S(1)}, u32[]{:S(2)}, u32[]{:S(2)}) async-start(f32[1,1,256,256]{3,1,0,2:T(1,128)} %copy.208), calls=%async_computation.4 | async-start | bytes 524288 | tf_op jit(solution)/shard_map/all_to_all | solution.py:83
  114.4 21.5 %all-to-all-start = ((f32[2,1,256,256]{3,0,1,2:T(2,128)}), f32[2,1,256,256]{3,0,1,2:T(2,128)S(1)}, u32[]{:S(2)}, u32[]{:S(2)}) async-start(f32[2,1,256,256]{3,0,1,2:T(2,128)} %copy.166), calls=%async_computation | async-start | bytes 1048576 | tf_op jit(solution)/shard_map/all_to_all | solution.py:83
  135.9 34.0 %all-to-all-start.5 = ((f32[2,1,32,2,8,256]{5,3,4,1,0,2:T(2,128)}), f32[2,1,32,2,8,256]{5,3,4,1,0,2:T(2,128)}, u32[]{:S(2)}, u32[]{:S(2)}) async-start(f32[2,1,32,2,8,256]{5,3,4,1,0,2:T(2,128)} %copy.259), calls=%async_computation.5 | async-start | bytes 2097152 | tf_op jit(solution)/shard_map/all_to_all | solution.py:95
  145.7 1.6 copy-start.3
  169.9 54.6 %all-to-all-start.1 = ((f32[2,2,32,2,8,256]{5,3,4,1,0,2:T(2,128)}), f32[2,2,32,2,8,256]{5,3,4,1,0,2:T(2,128)S(1)}, u32[]{:S(2)}, u32[]{:S(2)}) async-start(f32[2,2,32,2,8,256]{5,3,4,1,0,2:T(2,128)} %copy.256), calls=%async_computation.1 | async-start | bytes 4194304 | tf_op jit(solution)/shard_map/all_to_all | solution.py:95
  176.5 3.3 copy-start.5
  242.3 1.0 copy-start.6
  242.3 1.2 copy-start.7
  277.9 34.4 %all-to-all-start.2 = ((f32[32,2,1,1,2,1,8,256]{7,6,4,1,5,3,2,0:T(8,128)}), f32[32,2,1,1,2,1,8,256]{7,6,4,1,5,3,2,0:T(8,128)}, u32[]{:S(2)}, u32[]{:S(2)}) async-start(f32[32,2,1,1,2,1,8,256]{7,6,4,1,5,3,2,0:T(8,128)} %constant_dynamic-update-slice_fusion), calls=%async_computation.2 | async-start | bytes 2097152 | tf_op jit(solution)/shard_map/all_to_all | solution.py:12
  284.1 3.4 copy-start.2
  290.2 1.4 copy-start.4
  312.3 54.6 %all-to-all-start.6 = ((f32[32,2,2,1,2,1,8,256]{7,6,4,2,1,5,3,0:T(8,128)}), f32[32,2,2,1,2,1,8,256]{7,6,4,2,1,5,3,0:T(8,128)S(1)}, u32[]{:S(2)}, u32[]{:S(2)}) async-start(f32[32,2,2,1,2,1,8,256]{7,6,4,2,1,5,3,0:T(8,128)} %copy-done.4), calls=%async_computation.6 | async-start | bytes 4194304 | tf_op jit(solution)/shard_map/all_to_all | solution.py:12
  366.9 20.3 %all-to-all-start.3 = ((f32[1,32,8,256]{3,2,0,1:T(8,128)}), f32[1,32,8,256]{3,2,0,1:T(8,128)S(1)}, u32[]{:S(2)}, u32[]{:S(2)}) async-start(f32[1,32,8,256]{3,2,0,1:T(8,128)} %copy.207), calls=%async_computation.3 | async-start | bytes 524288 | tf_op jit(solution)/shard_map/all_to_all | solution.py:111
  385.4 11.8 %copy-start.14 = (f32[8]{0:T(128)S(1)}, f32[8]{0:T(128)}, u32[]{:S(2)}) copy-start(f32[8]{0:T(128)} %param.12) | copy-start | bytes 100
  385.4 87.7 %copy-start.1 = (f32[3,256,256]{2,1,0:T(8,128)S(1)}, f32[3,256,256]{2,1,0:T(8,128)}, u32[]{:S(2)}) copy-start(f32[3,256,256]{2,1,0:T(8,128)} %copy-done) | copy-start | bytes 2359300
  385.4 87.7 %copy-start.12 = (bf16[256,256]{1,0:T(8,128)(2,1)S(1)}, bf16[256,256]{1,0:T(8,128)(2,1)}, u32[]{:S(2)}) copy-start(bf16[256,256]{1,0:T(8,128)(2,1)} %param.13) | copy-start | bytes 393220
  387.2 85.9 %all-to-all-start.7 = ((f32[2,32,8,256]{3,2,0,1:T(8,128)}), f32[2,32,8,256]{3,2,0,1:T(8,128)S(1)}, u32[]{:S(2)}, u32[]{:S(2)}) async-start(f32[2,32,8,256]{3,2,0,1:T(8,128)} %copy.248), calls=%async_computation.7 | async-start | bytes 1048576 | tf_op jit(solution)/shard_map/all_to_all | solution.py:111
  474.0 5.5 collective-permute-start.1
